TPU v7x, 256 devices: a whole 4x4x8 slice. The times are simulated.
256 devices in a mesh: px: 16 (over z, y_hi), py: 16 (over x, y_lo, core).
Axes of the slice: x: 4, y: 4 (y_hi: 2, y_lo: 2; y = y_hi * 2 + y_lo), z: 8, core: 2. Of those that a mesh axis runs over, the one named last changes fastest.
Arguments:
- estimate: float32 [512, 512, 128], P('px', 'py'), may hold values from 0.2 to 5
- observed: float32 [512, 512, 128], P('px', 'py'), may hold values from 0.2 to 5
- psf: float32 [32, 32, 32], replicated, as said below
Outputs:
- updated: float32 [512, 512, 128], P('px', 'py')
Inputs may be any that keep to these rules, and one draw needn't show every extreme that they name: `psf`: every entry is positive.
All inputs are finite; a program needn't handle non-finite values.
Results may differ from a plain program's by a relative error of at most 0.00009.
Values sent between devices are 32-bit elements; how exact they have to be, the bound alone decides.
No kernel may reach another device: no remote copies, remote signals or barrier semaphores. Data moves between devices by JAX's collectives and lax.ppermute only.
A program may use at most 128 MiB of HBM per device.

v0:
```python
import math
import jax
import jax.numpy as jnp
from jax import lax
from jax.sharding import PartitionSpec as P

NX = 512
NY = 512
penalty_weight = 0.1
smoothing = 0.1


def with_halo(block, sides, width):
    for axis, dim in sides:
        count = lax.axis_size(axis)
        forward = [(i, i + 1) for i in range(count - 1)]
        backward = [(target, source) for source, target in forward]
        low = lax.ppermute(
            lax.slice_in_dim(block, block.shape[dim] - width, None, axis=dim), axis, forward
        )
        high = lax.ppermute(lax.slice_in_dim(block, 0, width, axis=dim), axis, backward)
        block = jnp.concatenate([low, block, high], axis=dim)
    return block


def product(pattern, left, right):
    return jnp.einsum(pattern, left, right, precision=lax.Precision.HIGHEST)


def tables(length):
    indices = jnp.arange(length)
    turns = jnp.remainder(indices[:, None] * indices[None, :], length).astype(jnp.float32) * (
        2.0 * math.pi / length
    )
    return (jnp.cos(turns), jnp.sin(turns))


def offset_tables(offsets, frequency, length):
    turns = jnp.remainder(offsets[:, None] * frequency[None, :], length).astype(jnp.float32) * (
        2.0 * math.pi / length
    )
    return (jnp.cos(turns), jnp.sin(turns))


def complex_apply(real_part, imag_part, cosine, sines, pattern, forward):
    real_cos = product(pattern, real_part, cosine)
    real_sin = product(pattern, real_part, sines)
    imag_cos = product(pattern, imag_part, cosine)
    imag_sin = product(pattern, imag_part, sines)
    if forward:
        return (real_cos + imag_sin, imag_cos - real_sin)
    return (real_cos - imag_sin, imag_cos + real_sin)


def transfer_function(
    kernel, first_index, second_index, depth_share, first_share, second_whole, first_whole, depth
):
    length = kernel.shape[0]
    offsets = jnp.arange(length) - length // 2
    depth_freq = first_index * depth_share + jnp.arange(depth_share)
    first_freq = second_index * first_share + jnp.arange(first_share)
    second_freq = jnp.arange(second_whole)
    cosine, sines = offset_tables(offsets, depth_freq, depth)
    real_part = product("baz,zk->bak", kernel, cosine)
    imag_part = -product("baz,zk->bak", kernel, sines)
    cosine, sines = offset_tables(offsets, first_freq, first_whole)
    real_part, imag_part = complex_apply(real_part, imag_part, cosine, sines, "baz,aj->bzj", True)
    cosine, sines = offset_tables(offsets, second_freq, second_whole)
    real_part, imag_part = complex_apply(real_part, imag_part, cosine, sines, "bzj,bm->zjm", True)
    factor = 1.0 / (first_whole * second_whole * depth)
    return (real_part * factor, imag_part * factor)


def outward_one(spectrum, handler):
    result = handler(lax.all_to_all(spectrum, "py", split_axis=2, concat_axis=3, tiled=True))
    return result


def outward_two(spectrum):
    result = lax.all_to_all(spectrum, "px", split_axis=2, concat_axis=3, tiled=True)
    return result


def homeward_two(spectrum, handler):
    result = handler(lax.all_to_all(spectrum, "px", split_axis=3, concat_axis=2, tiled=True))
    return result


def homeward_one(spectrum, handler):
    result = handler(lax.all_to_all(spectrum, "py", split_axis=3, concat_axis=2, tiled=True))
    return result


def along_first(segment):
    cosine, sines = tables(segment.shape[3])
    real_part, imag_part = complex_apply(segment[0], segment[1], cosine, sines, "bza,ak->zkb", True)
    return jnp.stack([real_part, imag_part])


def inverse_first(segment):
    cosine, sines = tables(segment.shape[2])
    real_part, imag_part = complex_apply(
        segment[0], segment[1], cosine, sines, "zab,ak->bzk", False
    )
    return jnp.stack([real_part, imag_part])


def to_real(segment):
    cosine, sines = tables(segment.shape[2])
    return product("bza,zk->bak", segment[0], cosine) - product("bza,zk->bak", segment[1], sines)


def convolve(volume, transfer_real, transfer_imag, adjoint):
    cosine, sines = tables(volume.shape[2])
    spectrum = jnp.stack(
        [product("baz,zk->bka", volume, cosine), -product("baz,zk->bka", volume, sines)]
    )
    spectrum = outward_one(spectrum, along_first)
    spectrum = outward_two(spectrum)
    cosine_second, sines_second = tables(spectrum.shape[3])
    real_part, imag_part = complex_apply(
        spectrum[0], spectrum[1], cosine_second, sines_second, "zab,bk->zak", True
    )
    signed_imag = -transfer_imag if adjoint else transfer_imag
    weighted_real = real_part * transfer_real - imag_part * signed_imag
    weighted_imag = real_part * signed_imag + imag_part * transfer_real
    real_part, imag_part = complex_apply(
        weighted_real, weighted_imag, cosine_second, sines_second, "zab,bk->zak", False
    )
    spectrum = homeward_two(jnp.stack([real_part, imag_part]), inverse_first)
    return homeward_one(spectrum, to_real)


def backward_depth(flux):
    return flux - jnp.concatenate([jnp.zeros_like(flux[:, :, :1]), flux[:, :, :-1]], 2)


def normalized(slope_rows, slope_cols, slope_depth):
    factor = lax.rsqrt(
        slope_rows * slope_rows
        + slope_cols * slope_cols
        + slope_depth * slope_depth
        + smoothing * smoothing
    )
    return (slope_rows * factor, slope_cols * factor, slope_depth * factor)


def variation(volume):
    row_count = volume.shape[0]
    col_count = volume.shape[1]
    padded = with_halo(volume, (("px", 0), ("py", 1)), 1)
    region = padded[:-1, :-1]
    slope_rows = padded[1:, :-1] - region
    slope_cols = padded[:-1, 1:] - region
    row_global = lax.axis_index("px") * row_count - 1 + jnp.arange(row_count + 1)
    col_global = lax.axis_index("py") * col_count - 1 + jnp.arange(col_count + 1)
    row_valid = ((row_global >= 0) & (row_global <= NX - 2))[:, None, None]
    col_valid = ((col_global >= 0) & (col_global <= NY - 2))[None, :, None]
    slope_rows = jnp.where(row_valid, slope_rows, 0.0)
    slope_cols = jnp.where(col_valid, slope_cols, 0.0)
    slope_depth = jnp.concatenate(
        [region[:, :, 1:] - region[:, :, :-1], jnp.zeros_like(region[:, :, :1])], 2
    )
    flux_rows, flux_cols, flux_depth = normalized(slope_rows, slope_cols, slope_depth)
    divergence = (
        flux_rows[1:, 1:]
        - flux_rows[:-1, 1:]
        + (flux_cols[1:, 1:] - flux_cols[1:, :-1])
        + backward_depth(flux_depth[1:, 1:])
    )
    return divergence


def shards(estimate, observed, psf):
    first_index = lax.axis_index("py")
    second_index = lax.axis_index("px")
    first_size = lax.axis_size("py")
    second_size = lax.axis_size("px")
    second_local, first_local, depth = estimate.shape
    first_whole = first_local * first_size
    second_whole = second_local * second_size
    transfer_real, transfer_imag = transfer_function(
        psf,
        first_index,
        second_index,
        depth // first_size,
        first_whole // second_size,
        second_whole,
        first_whole,
        depth,
    )
    blurred = convolve(estimate, transfer_real, transfer_imag, False)
    quotient = observed / blurred
    correction = convolve(quotient, transfer_real, transfer_imag, True)
    divergence = variation(estimate)
    return estimate * correction / (1.0 - penalty_weight * divergence)


def solution(mesh):
    placed = (P("px", "py", None), P("px", "py", None), P())
    return jax.shard_map(
        shards, mesh=mesh, in_specs=placed, out_specs=P("px", "py", None), check_vma=False
    )
```

profile of v0, /device:TPU:2, one launch (start us, length us, event | category | flops | bytes accessed | tf_op | source)
XLA Modules:
  0.0 613.5 jit_solution(9039552779921789667)
XLA Ops:
  13.1 6.1 all-to-all-start
  21.4 12.0 %all-to-all-done = f32[16,1,16384]{2,1,0:T(1,128)S(1)} async-done(((f32[16,1,16384]{2,1,0:T(1,128)}), f32[16,1,16384]{2,1,0:T(1,128)S(1)}, u32[]{:S(2)}, u32[]{:S(2)}) %all-to-all-start) | async-done | bytes 1048608 | tf_op jit(solution)/shard_map/all_to_all | solution.py:75
  47.5 6.0 fusion.59
  55.6 6.5 %fusion.57 = f32[512,32,8]{0,1,2:T(8,128)S(1)} fusion(f32[32,8,512]{2,0,1:T(8,128)} %squeeze.49), kind=kOutput, calls=%fused_computation.103 | convolution fusion | flops 808976384 | bytes 1048576 | tf_op jit(solution)/shard_map/bza,ak->zkb/dot_general | solution.py:27
  81.4 11.3 %all-to-all-start.1 = ((f32[16,1,16384]{2,1,0:T(1,128)}), f32[16,1,16384]{2,1,0:T(1,128)S(1)}, u32[]{:S(2)}, u32[]{:S(2)}) async-start(f32[16,1,16384]{2,1,0:T(1,128)} %reshape.86), calls=%async_computation.1 | async-start | bytes 2097152 | tf_op jit(solution)/shard_map/all_to_all | solution.py:80
  101.6 20.9 %all-to-all-done.1 = f32[16,1,16384]{2,1,0:T(1,128)S(1)} async-done(((f32[16,1,16384]{2,1,0:T(1,128)}), f32[16,1,16384]{2,1,0:T(1,128)S(1)}, u32[]{:S(2)}, u32[]{:S(2)}) %all-to-all-start.1) | async-done | bytes 1048608 | tf_op jit(solution)/shard_map/all_to_all | solution.py:80
  137.2 5.8 fusion.55
  154.6 5.7 multiply_subtract_fusion.1
  176.3 5.8 fusion.8
  189.7 33.3 %all_to_all.120 = f32[16,1,16384]{2,1,0:T(1,128)S(1)} all-to-all(f32[16,1,16384]{2,1,0:T(1,128)S(1)} %reshape.88), channel_id=1, replica_groups=mesh['px'=16,'py'=16] {'px'}, dimensions={0} | all-to-all | bytes 2097152 | tf_op jit(solution)/shard_map/all_to_all | solution.py:85
  237.6 5.9 fusion.109
  243.5 5.5 fusion.91
  255.2 5.4 fusion.111
  268.4 19.6 %all_to_all.121 = f32[16,1,16384]{2,1,0:T(1,128)S(1)} all-to-all(f32[16,1,16384]{2,1,0:T(1,128)S(1)} %reshape.90), channel_id=1, replica_groups=mesh['px'=16,'py'=16] {'py'}, dimensions={0} | all-to-all | bytes 2097152 | tf_op jit(solution)/shard_map/all_to_all | solution.py:90
  294.0 6.2 %copy.73 = f32[2,32,8,16,32]{4,2,3,1,0:T(8,128)} copy(f32[2,32,8,16,32]{1,2,0,4,3:T(8,128)} %bitcast.349) | data formatting | bytes 2097152 | tf_op jit(solution)/shard_map/all_to_all | solution.py:90
  320.4 19.2 %all_to_all.122 = f32[16,1,16384]{2,1,0:T(1,128)S(1)} all-to-all(f32[16,1,16384]{2,1,0:T(1,128)S(1)} %reshape.92), channel_id=1, replica_groups=mesh['px'=16,'py'=16] {'py'}, dimensions={0} | all-to-all | bytes 2097152 | tf_op jit(solution)/shard_map/all_to_all | solution.py:75
  353.1 5.9 fusion.47
  360.2 5.6 fusion.45
  384.2 34.2 %all_to_all.123 = f32[16,1,16384]{2,1,0:T(1,128)S(1)} all-to-all(f32[16,1,16384]{2,1,0:T(1,128)S(1)} %reshape.94), channel_id=1, replica_groups=mesh['px'=16,'py'=16] {'px'}, dimensions={0} | all-to-all | bytes 2097152 | tf_op jit(solution)/shard_map/all_to_all | solution.py:80
  433.0 5.8 fusion.43
  439.6 5.5 fusion.41
  450.5 5.5 multiply_subtract_fusion
  461.3 5.5 fusion.37
  496.4 5.7 collective-permute-done.1
  502.9 16.5 %all-to-all-done.6 = f32[16,1,16384]{2,1,0:T(1,128)S(1)} async-done(((f32[16,1,16384]{2,1,0:T(1,128)}), f32[16,1,16384]{2,1,0:T(1,128)S(1)}, u32[]{:S(2)}, u32[]{:S(2)}) %all-to-all-start.6) | async-done | bytes 1048608 | tf_op jit(solution)/shard_map/all_to_all | solution.py:85
  534.4 5.9 fusion.113
  540.2 5.8 fusion.95
  546.9 5.5 fusion.93
  552.5 5.4 fusion.115
  577.7 7.7 %collective-permute-done.2 = f32[34,1,128]{2,1,0:T(1,128)S(1)} collective-permute-done((f32[34,1,128]{2,1,0:T(1,128)S(1)}, f32[34,1,128]{2,1,0:T(1,128)S(1)}, u32[]{:S(2)}, u32[]{:S(2)}) %collective-permute-start.2) | collective-permute-done | bytes 17440 | tf_op jit(solution)/shard_map/ppermute | solution.py:18
  595.9 6.1 copy.85
  607.1 6.2 %fusion.19 = f32[32,32,128]{2,1,0:T(8,128)} fusion(f32[32,32,128]{2,1,0:T(8,128)S(1)} %copy-done.2, f32[32,32,128]{2,1,0:T(8,128)S(1)} %fusion, f32[2,32,16,8,32]{4,3,2,1,0:T(8,128)} %bitcast.355, f32[33,33,128]{2,1,0:T(8,128)S(1)} %get-tuple-element.25, f32[33,33,128]{2,1,0:T(8,128)S(1)} %get-tuple-element.24, f32[33,33,128]{2,1,0:T(8,128)S(1)} %copy-done.7, ...), kind=kOutput, calls=%fused_computation.53 | convolution fusion | flops 202866688 | bytes 6815744 | tf_op jit(solution)/shard_map/bza,zk->bak/dot_general | solution.py:27
  (167 shorter events, 304.4 us)
Async XLA Ops:
  0.0 19.2 %copy-start = (f32[32,32,32]{2,1,0:T(8,128)S(1)}, f32[32,32,32]{2,1,0:T(8,128)}, u32[]{:S(2)}) copy-start(f32[32,32,32]{2,1,0:T(8,128)} %param.5) | copy-start | bytes 393220
  13.1 20.4 %all-to-all-start = ((f32[16,1,16384]{2,1,0:T(1,128)}), f32[16,1,16384]{2,1,0:T(1,128)S(1)}, u32[]{:S(2)}, u32[]{:S(2)}) async-start(f32[16,1,16384]{2,1,0:T(1,128)} %reshape.84), calls=%async_computation | async-start | bytes 2097152 | tf_op jit(solution)/shard_map/all_to_all | solution.py:75
  47.5 6.1 copy-start.3
  55.6 6.5 %copy-start.12 = (f32[32,8,512]{2,0,1:T(8,128)S(1)}, f32[32,8,512]{2,0,1:T(8,128)}, u32[]{:S(2)}) copy-start(f32[32,8,512]{2,0,1:T(8,128)} %squeeze.49) | copy-start | bytes 1572868
  55.6 6.5 %copy-start.17 = (f32[512,32,8]{0,1,2:T(8,128)S(1)}, f32[512,32,8]{0,1,2:T(8,128)}, u32[]{:S(2)}) copy-start(f32[512,32,8]{0,1,2:T(8,128)} %fusion.59) | copy-start | bytes 1572868
  81.4 41.2 %all-to-all-start.1 = ((f32[16,1,16384]{2,1,0:T(1,128)}), f32[16,1,16384]{2,1,0:T(1,128)S(1)}, u32[]{:S(2)}, u32[]{:S(2)}) async-start(f32[16,1,16384]{2,1,0:T(1,128)} %reshape.86), calls=%async_computation.1 | async-start | bytes 2097152 | tf_op jit(solution)/shard_map/all_to_all | solution.py:80
  143.8 5.4 copy-start.19
  143.8 10.7 %copy-start.13 = (f32[8,32,512]{2,1,0:T(8,128)S(1)}, f32[8,32,512]{2,1,0:T(8,128)}, u32[]{:S(2)}) copy-start(f32[8,32,512]{2,1,0:T(8,128)} %fusion.16) | copy-start | bytes 1572868
  143.9 10.7 %copy-start.15 = (f32[8,32,512]{2,1,0:T(8,128)S(1)}, f32[8,32,512]{2,1,0:T(8,128)}, u32[]{:S(2)}) copy-start(f32[8,32,512]{2,1,0:T(8,128)} %fusion.17) | copy-start | bytes 1572868
  249.8 10.8 %copy-start.10 = (f32[512,256]{0,1:S(1)}, f32[512,256]{0,1}, u32[]{:S(2)}) copy-start(f32[512,256]{0,1} %fusion.109) | copy-start | bytes 1572868
  294.0 11.2 %copy-start.8 = (f32[32,32,128]{2,1,0:T(8,128)S(1)}, f32[32,32,128]{2,1,0:T(8,128)}, u32[]{:S(2)}) copy-start(f32[32,32,128]{2,1,0:T(8,128)} %param.4) | copy-start | bytes 1572868
  353.1 5.9 copy-start.4
  360.2 5.6 copy-start.18
  439.6 5.5 copy-start.20
  439.6 10.9 %copy-start.14 = (f32[8,32,512]{2,1,0:T(8,128)S(1)}, f32[8,32,512]{2,1,0:T(8,128)}, u32[]{:S(2)}) copy-start(f32[8,32,512]{2,1,0:T(8,128)} %fusion.16) | copy-start | bytes 1572868
  439.6 10.9 %copy-start.16 = (f32[8,32,512]{2,1,0:T(8,128)S(1)}, f32[8,32,512]{2,1,0:T(8,128)}, u32[]{:S(2)}) copy-start(f32[8,32,512]{2,1,0:T(8,128)} %fusion.17) | copy-start | bytes 1572868
  481.3 8.4 %copy-start.2 = (f32[32,32,128]{2,1,0:T(8,128)S(1)}, f32[32,32,128]{2,1,0:T(8,128)}, u32[]{:S(2)}) copy-start(f32[32,32,128]{2,1,0:T(8,128)} %param.3) | copy-start | bytes 1572868
  486.1 33.3 %all-to-all-start.6 = ((f32[16,1,16384]{2,1,0:T(1,128)}), f32[16,1,16384]{2,1,0:T(1,128)S(1)}, u32[]{:S(2)}, u32[]{:S(2)}) async-start(f32[16,1,16384]{2,1,0:T(1,128)} %reshape.96), calls=%async_computation.6 | async-start | bytes 2097152 | tf_op jit(solution)/shard_map/all_to_all | solution.py:85
  489.8 6.6 %collective-permute-start = (f32[1,32,128]{2,1,0:T(8,128)S(1)}, f32[1,32,128]{2,1,0:T(8,128)S(1)}, u32[]{:S(2)}, u32[]{:S(2)}) collective-permute-start(f32[1,32,128]{2,1,0:T(8,128)S(1)} %get-tuple-element.29), channel_id=1, source_target_pairs={{0,16},{16,32},{32,48},{48,64},{64,80},{80,96},{96,112},{112,128},... | collective-permute-start | bytes 49160 | tf_op jit(solution)/shard_map/ppermute | solution.py:18
  495.0 7.1 %collective-permute-start.1 = (f32[1,32,128]{2,1,0:T(8,128)S(1)}, f32[1,32,128]{2,1,0:T(8,128)S(1)}, u32[]{:S(2)}, u32[]{:S(2)}) collective-permute-start(f32[1,32,128]{2,1,0:T(8,128)S(1)} %get-tuple-element.28), channel_id=1, source_target_pairs={{16,0},{32,16},{48,32},{64,48},{80,64},{96,80},{112,96},{128,112},... | collective-permute-start | bytes 49160 | tf_op jit(solution)/shard_map/ppermute | solution.py:21
  502.1 0.8 copy-start.5
  546.9 11.0 %copy-start.11 = (f32[512,256]{0,1:S(1)}, f32[512,256]{0,1}, u32[]{:S(2)}) copy-start(f32[512,256]{0,1} %fusion.113) | copy-start | bytes 1572868
  552.4 5.5 copy-start.9
  561.8 9.4 %copy-start.6 = (f32[34,32,128]{2,1,0:T(8,128)S(1)}, f32[34,32,128]{2,1,0:T(8,128)}, u32[]{:S(2)}) copy-start(f32[34,32,128]{2,1,0:T(8,128)} %copy-done.5) | copy-start | bytes 1671172
  566.6 21.7 %all-to-all-start.7 = ((f32[16,1,16384]{2,1,0:T(1,128)}), f32[16,1,16384]{2,1,0:T(1,128)}, u32[]{:S(2)}, u32[]{:S(2)}) async-start(f32[16,1,16384]{2,1,0:T(1,128)} %reshape.98), calls=%async_computation.7 | async-start | bytes 2097152 | tf_op jit(solution)/shard_map/all_to_all | solution.py:90
  571.2 14.2 %collective-permute-start.2 = (f32[34,1,128]{2,1,0:T(1,128)S(1)}, f32[34,1,128]{2,1,0:T(1,128)S(1)}, u32[]{:S(2)}, u32[]{:S(2)}) collective-permute-start(f32[34,1,128]{2,1,0:T(1,128)S(1)} %get-tuple-element.27), channel_id=1, source_target_pairs={{0,1},{1,2},{2,3},{3,4},{4,5},{5,6},{6,7},{7,8},{8,9},{9,10},{10,1... | collective-permute-start | bytes 52232 | tf_op jit(solution)/shard_map/ppermute | solution.py:18
  573.3 12.4 %collective-permute-start.3 = (f32[34,1,128]{2,1,0:T(1,128)S(1)}, f32[34,1,128]{2,1,0:T(1,128)S(1)}, u32[]{:S(2)}, u32[]{:S(2)}) collective-permute-start(f32[34,1,128]{2,1,0:T(1,128)S(1)} %get-tuple-element.26), channel_id=1, source_target_pairs={{1,0},{2,1},{3,2},{4,3},{5,4},{6,5},{7,6},{8,7},{9,8},{10,9},{11,1... | collective-permute-start | bytes 52232 | tf_op jit(solution)/shard_map/ppermute | solution.py:21
  595.9 11.2 %copy-start.7 = (f32[33,33,128]{2,1,0:T(8,128)S(1)}, f32[33,33,128]{2,1,0:T(8,128)}, u32[]{:S(2)}) copy-start(f32[33,33,128]{2,1,0:T(8,128)} %get-tuple-element.5) | copy-start | bytes 1672708
  601.9 11.3 %copy-start.1 = (f32[32,32,32]{2,1,0:T(8,128)S(1)}, f32[32,32,32]{2,1,0:T(8,128)}, u32[]{:S(2)}) copy-start(f32[32,32,32]{2,1,0:T(8,128)} %param.5) | copy-start | bytes 393220
where the time goes:
time: 619 us; the launch traced here: 613 us
  matrix products  216 us (35%)
  local copies, waits for them, and re-layouts  159 us (26%)
  blocking collectives  106 us (17%)
  waiting for transfers between devices  62.9 us (10%)
  starting transfers between devices  38.6 us (6%)
  other arithmetic  29.9 us (5%)
    dot_general x42, matrix products, product(): return jnp.einsum(pattern, left, right, precision=lax.Precision.HIGHEST)  171 us
    unnamed x60, local copies, waits for them, and re-layouts  57.8 us
    unnamed x8, matrix products  44.8 us
    all_to_all x1, blocking collectives, outward_two(): lax.all_to_all(spectrum, 'px', split_axis=2, concat_axis=3, tiled=True)  34.2 us
    all_to_all x1, blocking collectives, homeward_two(): lax.all_to_all(spectrum, 'px', split_axis=3, concat_axis=2, tiled=True)  33.3 us
    all_to_all x1, waiting for transfers between devices, outward_two(): lax.all_to_all(spectrum, 'px', split_axis=2, concat_axis=3, tiled=True)  20.9 us
    all_to_all x1, blocking collectives, homeward_one(): lax.all_to_all(spectrum, 'py', split_axis=3, concat_axis=2, tiled=True)  19.6 us
    all_to_all x1, blocking collectives, outward_one(): lax.all_to_all(spectrum, 'py', split_axis=2, concat_axis=3, tiled=True)  19.2 us
  transfers between devices with their start and end apart: 8, of which 6 were waited for; matrix products, arithmetic and copies ran while one was open for 2% of the time, Pallas kernels for 0%

commit v1 on v0

--- a/solution.py
+++ b/solution.py
@@ -8,6 +8,13 @@
 NY = 512
 penalty_weight = 0.1
 smoothing = 0.1
+
+
+def swap_blocks(value, axis, split, join):
+    count = lax.axis_size(axis)
+    tiles = jnp.stack(jnp.split(value, count, axis=split), axis=0)
+    tiles = lax.all_to_all(tiles, axis, split_axis=0, concat_axis=0)
+    return jnp.concatenate(tiles, axis=join)
 
 
 def with_halo(block, sides, width):
@@ -77,7 +84,7 @@
 
 
 def outward_two(spectrum):
-    result = lax.all_to_all(spectrum, "px", split_axis=2, concat_axis=3, tiled=True)
+    result = swap_blocks(spectrum, "px", 2, 3)
     return result
 
 

time: 619 us -> 625 us (level)
    all_to_all x2 -> x0, local copies, waits for them, and re-layouts: 9.23 us -> none  [outward_two(): lax.all_to_all(spectrum, 'px', split_axis=2, concat_axis=3, tiled=True)]
    another operation x2 -> x0, local copies, waits for them, and re-layouts: 7.32 us -> none  [along_first(): return jnp.stack([real_part, imag_part])]
    unnamed x60 -> x66, local copies, waits for them, and re-layouts: 57.8 us -> 62.5 us
where the time goes in v1:
time: 625 us; the launch traced here: 619 us
  matrix products  218 us (35%)
  local copies, waits for them, and re-layouts  160 us (26%)
  blocking collectives  106 us (17%)
  waiting for transfers between devices  62.9 us (10%)
  starting transfers between devices  38.5 us (6%)
  other arithmetic  32.7 us (5%)
    dot_general x42, matrix products, product(): return jnp.einsum(pattern, left, right, precision=lax.Precision.HIGHEST)  172 us
    unnamed x66, local copies, waits for them, and re-layouts  62.5 us
    unnamed x8, matrix products  45.3 us
    all_to_all x1, blocking collectives, swap_blocks(): tiles = lax.all_to_all(tiles, axis, split_axis=0, concat_axis=0)  34.1 us
    all_to_all x1, blocking collectives, homeward_two(): lax.all_to_all(spectrum, 'px', split_axis=3, concat_axis=2, tiled=True)  33.3 us
    all_to_all x1, waiting for transfers between devices, swap_blocks(): tiles = lax.all_to_all(tiles, axis, split_axis=0, concat_axis=0)  20.9 us
    all_to_all x1, blocking collectives, outward_one(): lax.all_to_all(spectrum, 'py', split_axis=2, concat_axis=3, tiled=True)  19.4 us
    all_to_all x1, blocking collectives, homeward_one(): lax.all_to_all(spectrum, 'py', split_axis=3, concat_axis=2, tiled=True)  19.4 us
  transfers between devices with their start and end apart: 8, of which 6 were waited for; matrix products, arithmetic and copies ran while one was open for 2% of the time, Pallas kernels for 0%

profile of v1, /device:TPU:2, one launch (start us, length us, event | category | flops | bytes accessed | tf_op | source)
XLA Modules:
  0.0 619.2 jit_solution(11606695566176006822)
XLA Ops:
  13.1 6.2 %all-to-all-start = ((f32[16,1,16384]{2,1,0:T(1,128)}), f32[16,1,16384]{2,1,0:T(1,128)S(1)}, u32[]{:S(2)}, u32[]{:S(2)}) async-start(f32[16,1,16384]{2,1,0:T(1,128)} %reshape.94), calls=%async_computation | async-start | bytes 2097152 | tf_op jit(solution)/shard_map/all_to_all | solution.py:82
  21.6 12.0 %all-to-all-done = f32[16,1,16384]{2,1,0:T(1,128)S(1)} async-done(((f32[16,1,16384]{2,1,0:T(1,128)}), f32[16,1,16384]{2,1,0:T(1,128)S(1)}, u32[]{:S(2)}, u32[]{:S(2)}) %all-to-all-start) | async-done | bytes 1048608 | tf_op jit(solution)/shard_map/all_to_all | solution.py:82
  47.6 6.4 %fusion.57 = f32[512,32,8]{0,1,2:T(8,128)} fusion(f32[32,8,512]{2,0,1:T(8,128)S(1)} %squeeze.49), kind=kOutput, calls=%fused_computation.159 | convolution fusion | flops 808976384 | bytes 1048576 | tf_op jit(solution)/shard_map/bza,ak->zkb/dot_general | solution.py:34
  56.0 6.5 %fusion.59 = f32[512,32,8]{0,1,2:T(8,128)S(1)} fusion(f32[32,8,512]{2,0,1:T(8,128)} %squeeze.48), kind=kOutput, calls=%fused_computation.161 | convolution fusion | flops 808976384 | bytes 1048576 | tf_op jit(solution)/shard_map/bza,ak->zkb/dot_general | solution.py:34
  81.7 11.1 %all-to-all-start.1 = ((f32[16,1,16384]{2,1,0:T(1,128)}), f32[16,1,16384]{2,1,0:T(1,128)S(1)}, u32[]{:S(2)}, u32[]{:S(2)}) async-start(f32[16,1,16384]{2,1,0:T(1,128)} %reshape.96), calls=%async_computation.1 | async-start | bytes 2097152 | tf_op jit(solution)/shard_map/all_to_all | solution.py:16
  101.8 20.9 %all-to-all-done.1 = f32[16,1,16384]{2,1,0:T(1,128)S(1)} async-done(((f32[16,1,16384]{2,1,0:T(1,128)}), f32[16,1,16384]{2,1,0:T(1,128)S(1)}, u32[]{:S(2)}, u32[]{:S(2)}) %all-to-all-start.1) | async-done | bytes 1048608 | tf_op jit(solution)/shard_map/all_to_all | solution.py:16
  136.9 6.0 fusion.55
  156.8 5.5 multiply_subtract_fusion.1
  162.2 5.7 fusion.51
  191.8 33.3 %all_to_all.100 = f32[16,1,16384]{2,1,0:T(1,128)S(1)} all-to-all(f32[16,1,16384]{2,1,0:T(1,128)S(1)} %reshape.98), channel_id=1, replica_groups=mesh['px'=16,'py'=16] {'px'}, dimensions={0} | all-to-all | bytes 2097152 | tf_op jit(solution)/shard_map/all_to_all | solution.py:92
  239.6 5.9 fusion.109
  245.5 5.7 fusion.91
  257.4 5.4 fusion.111
  270.7 19.4 %all_to_all.101 = f32[16,1,16384]{2,1,0:T(1,128)S(1)} all-to-all(f32[16,1,16384]{2,1,0:T(1,128)S(1)} %reshape.100), channel_id=1, replica_groups=mesh['px'=16,'py'=16] {'py'}, dimensions={0} | all-to-all | bytes 2097152 | tf_op jit(solution)/shard_map/all_to_all | solution.py:97
  295.9 6.1 copy.69
  322.3 19.4 %all_to_all.102 = f32[16,1,16384]{2,1,0:T(1,128)S(1)} all-to-all(f32[16,1,16384]{2,1,0:T(1,128)S(1)} %reshape.102), channel_id=1, replica_groups=mesh['px'=16,'py'=16] {'py'}, dimensions={0} | all-to-all | bytes 2097152 | tf_op jit(solution)/shard_map/all_to_all | solution.py:82
  355.1 5.9 fusion.45
  363.0 5.5 fusion.47
  368.6 6.4 %fusion.6 = f32[1,8,512,32]{2,3,1,0:T(8,128)S(1)} fusion(f32[512,32,8]{0,1,2:T(8,128)S(1)} %copy-done.22, f32[32,8,512]{2,0,1:T(8,128)} %copy-done.15), kind=kOutput, calls=%fused_computation.85 | convolution fusion | flops 809107456 | bytes 1572864 | tf_op jit(solution)/shard_map/bza,ak->zkb/dot_general | solution.py:34
  388.0 34.1 %all_to_all.103 = f32[16,1,16384]{2,1,0:T(1,128)S(1)} all-to-all(f32[16,1,16384]{2,1,0:T(1,128)S(1)} %reshape.104), channel_id=1, replica_groups=mesh['px'=16,'py'=16] {'px'}, dimensions={0} | all-to-all | bytes 2097152 | tf_op jit(solution)/shard_map/all_to_all | solution.py:16
  436.3 5.8 fusion.43
  445.2 5.7 fusion.41
  456.3 5.5 multiply_subtract_fusion
  467.1 5.5 fusion.37
  502.2 5.7 collective-permute-done.1
  508.7 16.5 %all-to-all-done.6 = f32[16,1,16384]{2,1,0:T(1,128)S(1)} async-done(((f32[16,1,16384]{2,1,0:T(1,128)}), f32[16,1,16384]{2,1,0:T(1,128)S(1)}, u32[]{:S(2)}, u32[]{:S(2)}) %all-to-all-start.6) | async-done | bytes 1048608 | tf_op jit(solution)/shard_map/all_to_all | solution.py:92
  539.9 5.9 fusion.113
  545.8 5.8 fusion.95
  552.4 5.8 fusion.93
  583.6 7.7 %collective-permute-done.2 = f32[34,1,128]{2,1,0:T(1,128)S(1)} collective-permute-done((f32[34,1,128]{2,1,0:T(1,128)S(1)}, f32[34,1,128]{2,1,0:T(1,128)S(1)}, u32[]{:S(2)}, u32[]{:S(2)}) %collective-permute-start.2) | collective-permute-done | bytes 17440 | tf_op jit(solution)/shard_map/ppermute | solution.py:25
  601.6 6.1 copy.81
  612.9 6.2 fusion.19
  (205 shorter events, 308.4 us)
Async XLA Ops:
  0.0 19.3 %copy-start = (f32[32,32,32]{2,1,0:T(8,128)S(1)}, f32[32,32,32]{2,1,0:T(8,128)}, u32[]{:S(2)}) copy-start(f32[32,32,32]{2,1,0:T(8,128)} %param.5) | copy-start | bytes 393220
  13.1 20.5 %all-to-all-start = ((f32[16,1,16384]{2,1,0:T(1,128)}), f32[16,1,16384]{2,1,0:T(1,128)S(1)}, u32[]{:S(2)}, u32[]{:S(2)}) async-start(f32[16,1,16384]{2,1,0:T(1,128)} %reshape.94), calls=%async_computation | async-start | bytes 2097152 | tf_op jit(solution)/shard_map/all_to_all | solution.py:82
  47.6 6.4 %copy-start.3 = (f32[1,32,8,16,32]{4,2,3,1,0:T(8,128)S(1)}, f32[1,32,8,16,32]{4,2,3,1,0:T(8,128)}, u32[]{:S(2)}) copy-start(f32[1,32,8,16,32]{4,2,3,1,0:T(8,128)} %get-tuple-element.19) | copy-start | bytes 1572868
  56.0 6.5 %copy-start.14 = (f32[32,8,512]{2,0,1:T(8,128)S(1)}, f32[32,8,512]{2,0,1:T(8,128)}, u32[]{:S(2)}) copy-start(f32[32,8,512]{2,0,1:T(8,128)} %squeeze.48) | copy-start | bytes 1572868
  56.0 6.5 %copy-start.20 = (f32[512,32,8]{0,1,2:T(8,128)S(1)}, f32[512,32,8]{0,1,2:T(8,128)}, u32[]{:S(2)}) copy-start(f32[512,32,8]{0,1,2:T(8,128)} %fusion.57) | copy-start | bytes 1572868
  75.1 1.9 copy-start.5
  81.7 40.9 %all-to-all-start.1 = ((f32[16,1,16384]{2,1,0:T(1,128)}), f32[16,1,16384]{2,1,0:T(1,128)S(1)}, u32[]{:S(2)}, u32[]{:S(2)}) async-start(f32[16,1,16384]{2,1,0:T(1,128)} %reshape.96), calls=%async_computation.1 | async-start | bytes 2097152 | tf_op jit(solution)/shard_map/all_to_all | solution.py:16
  146.0 5.4 copy-start.21
  146.0 10.7 %copy-start.16 = (f32[8,32,512]{2,1,0:T(8,128)S(1)}, f32[8,32,512]{2,1,0:T(8,128)}, u32[]{:S(2)}) copy-start(f32[8,32,512]{2,1,0:T(8,128)} %fusion.16) | copy-start | bytes 1572868
  146.0 10.7 %copy-start.18 = (f32[8,32,512]{2,1,0:T(8,128)S(1)}, f32[8,32,512]{2,1,0:T(8,128)}, u32[]{:S(2)}) copy-start(f32[8,32,512]{2,1,0:T(8,128)} %fusion.17) | copy-start | bytes 1572868
  252.0 10.8 %copy-start.12 = (f32[512,256]{0,1:S(1)}, f32[512,256]{0,1}, u32[]{:S(2)}) copy-start(f32[512,256]{0,1} %fusion.109) | copy-start | bytes 1572868
  295.9 11.2 %copy-start.10 = (f32[32,32,128]{2,1,0:T(8,128)S(1)}, f32[32,32,128]{2,1,0:T(8,128)}, u32[]{:S(2)}) copy-start(f32[32,32,128]{2,1,0:T(8,128)} %param.4) | copy-start | bytes 1572868
  355.1 5.9 copy-start.4
  362.2 0.8 copy-start.15
  363.0 5.5 copy-start.22
  382.2 1.9 copy-start.6
  445.2 5.8 copy-start.23
  445.2 11.1 %copy-start.17 = (f32[8,32,512]{2,1,0:T(8,128)S(1)}, f32[8,32,512]{2,1,0:T(8,128)}, u32[]{:S(2)}) copy-start(f32[8,32,512]{2,1,0:T(8,128)} %fusion.16) | copy-start | bytes 1572868
  445.2 11.1 %copy-start.19 = (f32[8,32,512]{2,1,0:T(8,128)S(1)}, f32[8,32,512]{2,1,0:T(8,128)}, u32[]{:S(2)}) copy-start(f32[8,32,512]{2,1,0:T(8,128)} %fusion.17) | copy-start | bytes 1572868
  487.1 8.5 %copy-start.2 = (f32[32,32,128]{2,1,0:T(8,128)S(1)}, f32[32,32,128]{2,1,0:T(8,128)}, u32[]{:S(2)}) copy-start(f32[32,32,128]{2,1,0:T(8,128)} %param.3) | copy-start | bytes 1572868
  491.9 33.3 %all-to-all-start.6 = ((f32[16,1,16384]{2,1,0:T(1,128)}), f32[16,1,16384]{2,1,0:T(1,128)S(1)}, u32[]{:S(2)}, u32[]{:S(2)}) async-start(f32[16,1,16384]{2,1,0:T(1,128)} %reshape.106), calls=%async_computation.6 | async-start | bytes 2097152 | tf_op jit(solution)/shard_map/all_to_all | solution.py:92
  495.6 6.6 %collective-permute-start = (f32[1,32,128]{2,1,0:T(8,128)S(1)}, f32[1,32,128]{2,1,0:T(8,128)S(1)}, u32[]{:S(2)}, u32[]{:S(2)}) collective-permute-start(f32[1,32,128]{2,1,0:T(8,128)S(1)} %get-tuple-element.29), channel_id=1, source_target_pairs={{0,16},{16,32},{32,48},{48,64},{64,80},{80,96},{96,112},{112,128},... | collective-permute-start | bytes 49160 | tf_op jit(solution)/shard_map/ppermute | solution.py:25
  500.8 7.1 %collective-permute-start.1 = (f32[1,32,128]{2,1,0:T(8,128)S(1)}, f32[1,32,128]{2,1,0:T(8,128)S(1)}, u32[]{:S(2)}, u32[]{:S(2)}) collective-permute-start(f32[1,32,128]{2,1,0:T(8,128)S(1)} %get-tuple-element.28), channel_id=1, source_target_pairs={{16,0},{32,16},{48,32},{64,48},{80,64},{96,80},{112,96},{128,112},... | collective-permute-start | bytes 49160 | tf_op jit(solution)/shard_map/ppermute | solution.py:28
  507.9 0.8 copy-start.7
  552.4 11.2 %copy-start.13 = (f32[512,256]{0,1:S(1)}, f32[512,256]{0,1}, u32[]{:S(2)}) copy-start(f32[512,256]{0,1} %fusion.113) | copy-start | bytes 1572868
  558.2 5.5 copy-start.11
  567.6 9.4 %copy-start.8 = (f32[34,32,128]{2,1,0:T(8,128)S(1)}, f32[34,32,128]{2,1,0:T(8,128)}, u32[]{:S(2)}) copy-start(f32[34,32,128]{2,1,0:T(8,128)} %copy-done.7) | copy-start | bytes 1671172
  572.4 21.7 %all-to-all-start.7 = ((f32[16,1,16384]{2,1,0:T(1,128)}), f32[16,1,16384]{2,1,0:T(1,128)}, u32[]{:S(2)}, u32[]{:S(2)}) async-start(f32[16,1,16384]{2,1,0:T(1,128)} %reshape.108), calls=%async_computation.7 | async-start | bytes 2097152 | tf_op jit(solution)/shard_map/all_to_all | solution.py:97
  577.1 14.2 %collective-permute-start.2 = (f32[34,1,128]{2,1,0:T(1,128)S(1)}, f32[34,1,128]{2,1,0:T(1,128)S(1)}, u32[]{:S(2)}, u32[]{:S(2)}) collective-permute-start(f32[34,1,128]{2,1,0:T(1,128)S(1)} %get-tuple-element.27), channel_id=1, source_target_pairs={{0,1},{1,2},{2,3},{3,4},{4,5},{5,6},{6,7},{7,8},{8,9},{9,10},{10,1... | collective-permute-start | bytes 52232 | tf_op jit(solution)/shard_map/ppermute | solution.py:25
  579.1 12.4 %collective-permute-start.3 = (f32[34,1,128]{2,1,0:T(1,128)S(1)}, f32[34,1,128]{2,1,0:T(1,128)S(1)}, u32[]{:S(2)}, u32[]{:S(2)}) collective-permute-start(f32[34,1,128]{2,1,0:T(1,128)S(1)} %get-tuple-element.26), channel_id=1, source_target_pairs={{1,0},{2,1},{3,2},{4,3},{5,4},{6,5},{7,6},{8,7},{9,8},{10,9},{11,1... | collective-permute-start | bytes 52232 | tf_op jit(solution)/shard_map/ppermute | solution.py:28
  601.6 11.2 %copy-start.9 = (f32[33,33,128]{2,1,0:T(8,128)S(1)}, f32[33,33,128]{2,1,0:T(8,128)}, u32[]{:S(2)}) copy-start(f32[33,33,128]{2,1,0:T(8,128)} %get-tuple-element.5) | copy-start | bytes 1672708
  607.7 11.3 %copy-start.1 = (f32[32,32,32]{2,1,0:T(8,128)S(1)}, f32[32,32,32]{2,1,0:T(8,128)}, u32[]{:S(2)}) copy-start(f32[32,32,32]{2,1,0:T(8,128)} %param.5) | copy-start | bytes 393220
